TPU v7x, 32 devices: a whole 2x2x4 slice. The times are simulated.
32 devices in a mesh: blk: 2 (over x), head: 4 (over z), weight: 4 (over y, core).
Axes of the slice: x: 2, y: 2, z: 4, core: 2. Of those that a mesh axis runs over, the one named last changes fastest.
Arguments:
- hidden_in: bfloat16 [2048, 2, 768], P(('blk', 'head', 'weight')), may hold values from -6 to 6
- qkv_weight: bfloat16 [768, 2304], replicated, may hold values from -0.21875 to 0.21875
- query_bias: float32 [768], replicated, may hold values from -3 to 3
- value_bias: float32 [768], replicated, may hold values from -0.12 to 0.12
- out_weight: bfloat16 [768, 768], replicated, may hold values from -5.75 to 5.75
- out_bias: float32 [768], replicated, may hold values from -3 to 3
- norm1_gain: float32 [768], replicated, may hold values from 0.25 to 1.75
- norm1_bias: float32 [768], replicated, may hold values from -3 to 3
- up_weight: bfloat16 [768, 3072], P(None, 'weight'), may hold values from -0.21875 to 0.21875
- up_bias: float32 [3072], P('weight'), may hold values from -3 to 3
- down_weight: bfloat16 [3072, 768], P('weight'), may hold values from -0.109375 to 0.109375
- down_bias: float32 [768], replicated, may hold values from -3 to 3
- norm2_gain: float32 [768], replicated, may hold values from 0.25 to 1.75
- norm2_bias: float32 [768], replicated, may hold values from -3 to 3
- lengths: int32 [2], replicated, may hold values from 256 to 2048, as said below
- out_cotangent: bfloat16 [2048, 2, 768], P(('blk', 'head', 'weight')), may hold values from -6 to 6
Outputs:
- layer_out: bfloat16 [2048, 2, 768], P(('blk', 'head', 'weight'))
- grad_in: float32 [2048, 2, 768], P(('blk', 'head', 'weight'))
- grad_qkv_weight: float32 [768, 2304], replicated
- grad_query_bias: float32 [768], replicated
- grad_value_bias: float32 [768], replicated
- grad_out_weight: float32 [768, 768], replicated
- grad_out_bias: float32 [768], replicated
- grad_norm1_gain: float32 [768], replicated
- grad_norm1_bias: float32 [768], replicated
- grad_up_weight: float32 [768, 3072], P(None, 'weight')
- grad_up_bias: float32 [3072], P('weight')
- grad_down_weight: float32 [3072, 768], P('weight')
- grad_down_bias: float32 [768], replicated
- grad_norm2_gain: float32 [768], replicated
- grad_norm2_bias: float32 [768], replicated
Inputs may be any that keep to these rules, and one draw needn't show every extreme that they name: Positions 0 to lengths[b] - 1 of sequence b are tokens and the rest padding; at least one sequence has no padding.
All inputs are finite; a program needn't handle non-finite values.
Results may differ from a plain program's by a relative error of at most 0.02.
Values may be sent and summed in bfloat16 or wider, within the bound.
No kernel may reach another device: no remote copies, remote signals or barrier semaphores. Data moves between devices by JAX's collectives and lax.ppermute only.
A program may use at most 128 MiB of HBM per device.

v0:
```python
import jax
import jax.numpy as jnp
from jax import lax
from jax.sharding import PartitionSpec as P

HEADS = 12
HEAD_DIM = 64
EPS = 1e-05
SQRT_HALF = 0.7071067811865476
INV_ROOT_TAU = 0.3989422804014327


def norm_forward(resid, gain, bias):
    centre = jnp.mean(resid, axis=-1, keepdims=True)
    centred = resid - centre
    spread = jnp.mean(centred * centred, axis=-1, keepdims=True)
    rstd = lax.rsqrt(spread + EPS)
    normed = centred * rstd
    return (normed * gain + bias, normed, rstd)


def norm_backward(grad, normed, rstd, gain):
    scaled = grad * gain
    inner = (
        scaled
        - jnp.mean(scaled, axis=-1, keepdims=True)
        - normed * jnp.mean(scaled * normed, axis=-1, keepdims=True)
    )
    return (rstd * inner, jnp.sum(grad * normed, axis=0), jnp.sum(grad, axis=0))


def gelu_value(pre):
    return 0.5 * pre * (1.0 + jax.scipy.special.erf(pre * SQRT_HALF))


def gelu_slope(pre):
    return (
        0.5 * (1.0 + jax.scipy.special.erf(pre * SQRT_HALF))
        + pre * jnp.exp(-0.5 * pre * pre) * INV_ROOT_TAU
    )


def sweep(step, carry, piece):
    count = jax.tree.leaves(piece)[0].shape[0]
    size = 1024

    def advance(index, state):
        part = jax.tree.map(
            lambda leaf: lax.dynamic_slice_in_dim(leaf, index * size, size, 0), piece
        )
        return step(state, part, index * size)

    return lax.fori_loop(0, count // size, advance, carry)


def per_device(
    hidden_in,
    qkv_weight,
    query_bias,
    value_bias,
    out_weight,
    out_bias,
    norm1_gain,
    norm1_bias,
    up_weight,
    up_bias,
    down_weight,
    down_bias,
    norm2_gain,
    norm2_bias,
    lengths,
    out_cotangent,
):
    rows_here, seq_count, width = hidden_in.shape
    head_devs = lax.axis_size("head")
    weight_devs = lax.axis_size("weight")
    group = width // head_devs
    local_heads = HEADS // head_devs
    scale = HEAD_DIM ** (-0.5)
    tokens = rows_here * seq_count
    flat = hidden_in.reshape(tokens, width)
    bias_all = jnp.concatenate([query_bias, jnp.zeros((width,), jnp.float32), value_bias])
    packed = (jnp.dot(flat, qkv_weight, preferred_element_type=jnp.float32) + bias_all).astype(
        jnp.bfloat16
    )
    packed = packed.reshape(rows_here, seq_count, 3, width)
    regrouped = lax.all_to_all(packed, "head", split_axis=3, concat_axis=0, tiled=True)
    query_rows = regrouped.shape[0]
    query = regrouped[:, :, 0].reshape(query_rows, seq_count, local_heads, HEAD_DIM)
    keyval = regrouped[:, :, 1:]
    key_total = query_rows * lax.axis_size("blk") * weight_devs

    def positions(start, count):
        index = jnp.arange(count, dtype=jnp.int32) + start
        device = index // query_rows
        within = index % query_rows
        source = device // weight_devs * head_devs + within // rows_here
        return (source * weight_devs + device % weight_devs) * rows_here + within % rows_here

    def split_block(block, start):
        count = block.shape[0]
        keys = block[:, :, 0].reshape(count, seq_count, local_heads, HEAD_DIM)
        values = block[:, :, 1].reshape(count, seq_count, local_heads, HEAD_DIM)
        valid = positions(start, count)[None, :] < lengths[:, None]
        scores = (
            jnp.einsum("qbhe,kbhe->bhqk", query, keys, preferred_element_type=jnp.float32) * scale
        )
        weights = jnp.where(valid[:, None, None, :], jnp.exp(scores), 0.0)
        return (keys, values, weights)

    def forward_block(carry, block, start):
        numer, denom = carry
        keys, values, weights = split_block(block, start)
        numer = numer + jnp.einsum(
            "bhqk,kbhe->qbhe",
            weights.astype(jnp.bfloat16),
            values,
            preferred_element_type=jnp.float32,
        )
        return (numer, denom + jnp.sum(weights, axis=-1))

    first = (
        jnp.zeros((query_rows, seq_count, local_heads, HEAD_DIM), jnp.float32),
        jnp.zeros((seq_count, local_heads, query_rows), jnp.float32),
    )
    numer, denom = sweep(
        forward_block, first, lax.all_gather(keyval, ("blk", "weight"), axis=0, tiled=True)
    )
    attended = (numer / jnp.transpose(denom, (2, 0, 1))[..., None]).astype(jnp.bfloat16)
    returned = lax.all_to_all(
        attended.reshape(query_rows, seq_count, group),
        "head",
        split_axis=0,
        concat_axis=2,
        tiled=True,
    )
    attn_flat = returned.reshape(tokens, width)
    resid1 = (
        flat.astype(jnp.float32)
        + jnp.dot(attn_flat, out_weight, preferred_element_type=jnp.float32)
        + out_bias
    )
    hidden1, normed1, rstd1 = norm_forward(resid1, norm1_gain, norm1_bias)
    hidden_half = hidden1.astype(jnp.bfloat16).reshape(rows_here, seq_count, width)
    gathered = lax.all_gather(hidden_half, "weight", axis=0, tiled=True)
    gathered_flat = gathered.reshape(weight_devs * tokens, width)
    pre = jnp.dot(gathered_flat, up_weight, preferred_element_type=jnp.float32) + up_bias
    active = gelu_value(pre).astype(jnp.bfloat16)
    active_rows = active.reshape(weight_devs * rows_here, seq_count, -1)
    count = lax.axis_size("weight") * rows_here
    part = active_rows
    mixed = (
        lax.psum_scatter(
            jnp.dot(
                part.reshape(count * seq_count, -1), down_weight, preferred_element_type=jnp.float32
            )
            .reshape(count, seq_count, width)
            .astype(jnp.bfloat16),
            "weight",
            scatter_dimension=0,
            tiled=True,
        )
        .astype(jnp.float32)
        .reshape(tokens, width)
    )
    resid2 = hidden1 + mixed + down_bias
    final, normed2, rstd2 = norm_forward(resid2, norm2_gain, norm2_bias)
    layer_out = final.astype(jnp.bfloat16).reshape(rows_here, seq_count, width)
    cotangent = out_cotangent.reshape(tokens, width).astype(jnp.float32)
    grad_resid2, grad_norm2_gain, grad_norm2_bias = norm_backward(
        cotangent, normed2, rstd2, norm2_gain
    )
    grad_down_bias = jnp.sum(grad_resid2, axis=0)
    grad_mixed = grad_resid2.astype(jnp.bfloat16).reshape(rows_here, seq_count, width)
    mixed_all = lax.all_gather(grad_mixed, "weight", axis=0, tiled=True).reshape(
        weight_devs * tokens, width
    )
    grad_down_weight = jnp.dot(active.T, mixed_all, preferred_element_type=jnp.float32)
    grad_pre = jnp.dot(mixed_all, down_weight.T, preferred_element_type=jnp.float32) * gelu_slope(
        pre
    )
    grad_up_bias = jnp.sum(grad_pre, axis=0)
    grad_pre_half = grad_pre.astype(jnp.bfloat16)
    grad_up_weight = jnp.dot(gathered_flat.T, grad_pre_half, preferred_element_type=jnp.float32)
    pre_rows = grad_pre_half.reshape(weight_devs * rows_here, seq_count, -1)
    count = lax.axis_size("weight") * rows_here
    part = pre_rows
    back_hidden = (
        lax.psum_scatter(
            jnp.dot(
                part.reshape(count * seq_count, -1), up_weight.T, preferred_element_type=jnp.float32
            )
            .reshape(count, seq_count, width)
            .astype(jnp.bfloat16),
            "weight",
            scatter_dimension=0,
            tiled=True,
        )
        .astype(jnp.float32)
        .reshape(tokens, width)
    )
    grad_hidden1 = grad_resid2 + back_hidden
    grad_resid1, grad_norm1_gain, grad_norm1_bias = norm_backward(
        grad_hidden1, normed1, rstd1, norm1_gain
    )
    grad_out_bias = jnp.sum(grad_resid1, axis=0)
    grad_attn_half = grad_resid1.astype(jnp.bfloat16)
    grad_out_weight = jnp.dot(attn_flat.T, grad_attn_half, preferred_element_type=jnp.float32)
    grad_attended = jnp.dot(
        grad_attn_half, out_weight.T, preferred_element_type=jnp.float32
    ).astype(jnp.bfloat16)
    heads_grad = lax.all_to_all(
        grad_attended.reshape(rows_here, seq_count, width),
        "head",
        split_axis=2,
        concat_axis=0,
        tiled=True,
    )
    heads_grad = heads_grad.reshape(query_rows, seq_count, local_heads, HEAD_DIM)
    delta = jnp.transpose(
        jnp.sum(heads_grad.astype(jnp.float32) * attended.astype(jnp.float32), axis=-1), (1, 2, 0)
    )
    own_start = lax.axis_index(("blk", "weight")) * query_rows
    own_keys = keyval[:, :, 0].reshape(query_rows, seq_count, local_heads, HEAD_DIM)
    own_values = keyval[:, :, 1].reshape(query_rows, seq_count, local_heads, HEAD_DIM)
    own_valid = positions(own_start, query_rows)[None, :] < lengths[:, None]
    delta_rows = jnp.transpose(delta, (2, 0, 1))
    denom_rows = jnp.transpose(denom, (2, 0, 1))

    def key_side(carry, pieces, start):
        key_acc, value_acc, query_sums = carry
        query_piece, grad_piece, delta_piece, denom_piece = pieces
        count = query_piece.shape[0]
        scores = (
            jnp.einsum("qbhe,kbhe->bhqk", query_piece, own_keys, preferred_element_type=jnp.float32)
            * scale
        )
        weights = jnp.where(own_valid[:, None, None, :], jnp.exp(scores), 0.0)
        probs = weights / jnp.transpose(denom_piece, (1, 2, 0))[..., None]
        grad_prob = jnp.einsum(
            "qbhe,kbhe->bhqk", grad_piece, own_values, preferred_element_type=jnp.float32
        )
        score_half = (
            probs * (grad_prob - jnp.transpose(delta_piece, (1, 2, 0))[..., None])
        ).astype(jnp.bfloat16)
        value_acc = value_acc + jnp.einsum(
            "bhqk,qbhe->kbhe",
            probs.astype(jnp.bfloat16),
            grad_piece,
            preferred_element_type=jnp.float32,
        )
        key_acc = (
            key_acc
            + jnp.einsum(
                "bhqk,qbhe->kbhe", score_half, query_piece, preferred_element_type=jnp.float32
            )
            * scale
        )
        query_part = (
            jnp.einsum("bhqk,kbhe->qbhe", score_half, own_keys, preferred_element_type=jnp.float32)
            * scale
        )
        query_sums = lax.dynamic_update_slice_in_dim(
            query_sums, query_part.reshape(count, seq_count, group), start, 0
        )
        return (key_acc, value_acc, query_sums)

    second = (
        jnp.zeros((query_rows, seq_count, local_heads, HEAD_DIM), jnp.float32),
        jnp.zeros((query_rows, seq_count, local_heads, HEAD_DIM), jnp.float32),
        jnp.zeros((key_total, seq_count, group), jnp.float32),
    )
    key_acc, value_acc, query_sums = sweep(
        key_side,
        second,
        (
            lax.all_gather(query, ("blk", "weight"), axis=0, tiled=True),
            lax.all_gather(heads_grad, ("blk", "weight"), axis=0, tiled=True),
            lax.all_gather(
                delta_rows.astype(jnp.bfloat16), ("blk", "weight"), axis=0, tiled=True
            ).astype(jnp.float32),
            lax.all_gather(
                denom_rows.astype(jnp.bfloat16), ("blk", "weight"), axis=0, tiled=True
            ).astype(jnp.float32),
        ),
    )
    query_grad = lax.psum_scatter(
        query_sums.astype(jnp.bfloat16), ("blk", "weight"), scatter_dimension=0, tiled=True
    ).astype(jnp.float32)
    key_grad = key_acc.reshape(query_rows, seq_count, group)
    value_grad = value_acc.reshape(query_rows, seq_count, group)
    stacked = jnp.stack([query_grad, key_grad, value_grad], axis=2).astype(jnp.bfloat16)
    grad_packed = lax.all_to_all(stacked, "head", split_axis=0, concat_axis=3, tiled=True).reshape(
        tokens, 3 * width
    )
    grad_qkv_weight = jnp.dot(flat.T, grad_packed, preferred_element_type=jnp.float32)
    column_sums = jnp.sum(grad_packed.astype(jnp.float32), axis=0)
    grad_in = (
        jnp.dot(grad_packed, qkv_weight.T, preferred_element_type=jnp.float32) + grad_resid1
    ).reshape(rows_here, seq_count, width)
    shared = lax.psum(
        (
            grad_qkv_weight,
            column_sums[:width],
            column_sums[2 * width :],
            grad_out_weight,
            grad_out_bias,
            grad_norm1_gain,
            grad_norm1_bias,
            grad_norm2_gain,
            grad_norm2_bias,
            grad_down_bias,
        ),
        ("blk", "head", "weight"),
    )
    hidden_sums = (
        lax.psum(grad_up_weight.astype(jnp.bfloat16), ("blk", "head")).astype(jnp.float32),
        lax.psum(grad_up_bias.astype(jnp.bfloat16), ("blk", "head")).astype(jnp.float32),
        lax.psum(grad_down_weight.astype(jnp.bfloat16), ("blk", "head")).astype(jnp.float32),
    )
    return (
        layer_out,
        grad_in,
        shared[0],
        shared[1],
        shared[2],
        shared[3],
        shared[4],
        shared[5],
        shared[6],
        hidden_sums[0],
        hidden_sums[1],
        hidden_sums[2],
        shared[9],
        shared[7],
        shared[8],
    )


def solution(mesh):
    placed = (
        P(("blk", "head", "weight"), None, None),
        P(),
        P(),
        P(),
        P(),
        P(),
        P(),
        P(),
        P(None, "weight"),
        P("weight"),
        P("weight", None),
        P(),
        P(),
        P(),
        P(),
        P(("blk", "head", "weight"), None, None),
    )
    return jax.shard_map(
        per_device,
        mesh=mesh,
        in_specs=placed,
        out_specs=(
            P(("blk", "head", "weight"), None, None),
            P(("blk", "head", "weight"), None, None),
            P(),
            P(),
            P(),
            P(),
            P(),
            P(),
            P(),
            P(None, "weight"),
            P("weight"),
            P("weight", None),
            P(),
            P(),
            P(),
        ),
        check_vma=False,
    )
```

profile of v0, /device:TPU:0, one launch (start us, length us, event | category | flops | bytes accessed | tf_op | source)
XLA Modules:
  0.0 749.1 jit_solution(972970801593629136)
XLA Ops:
  14.1 4.8 copy.83
  21.6 22.3 %all_to_all.63 = bf16[4,2,36864]{2,1,0:T(2,128)(2,1)} all-to-all(bf16[4,2,36864]{2,1,0:T(2,128)(2,1)} %reshape.378), channel_id=1, replica_groups=mesh['blk'=2,'head'=4,'weight'=4] {'head'}, dimensions={0} | all-to-all | bytes 1179648 | tf_op jit(solution)/shard_map/all_to_all | solution.py:87
  46.6 4.8 copy.101
  58.3 32.0 %all-gather.4.cloned.1.call-done = bf16[2048,2,2,192]{3,0,2,1:T(8,128)(2,1)} async-done(((bf16[256,2,2,192]{3,0,2,1:T(8,128)(2,1)}), bf16[2048,2,2,192]{3,0,2,1:T(8,128)(2,1)}) %all-gather.4.cloned.1.call-update) | async-done | bytes 3145744 | tf_op jit(solution)/shard_map/all_gather | solution.py:127
  90.3 6.1 copy.87
  96.4 23.1 %while.37 = (s32[]{:T(128)}, f32[256,2,3,64]{0,3,2,1:T(8,128)}, f32[2,3,256]{2,1,0:T(4,128)S(1)}, bf16[2048,2,2,192]{0,3,1,2:T(8,128)(2,1)}, s32[2]{0:T(128)}, /...) while((s32[]{:T(128)}, f32[256,2,3,64]{0,3,2,1:T(8,128)}, ...), condition=%wide.region_2.3_spmd.clone, body=%wide.region_0.2_spmd.clone.sunk | while | flops 412356096 | bytes 19118340 | solution.py:53
  103.1 4.8 fusion.121
  114.6 4.9 fusion.121
  123.0 13.9 %all_to_all.64 = bf16[256,2,192]{2,1,0:T(2,128)(2,1)S(1)} all-to-all(bf16[256,2,192]{2,1,0:T(2,128)(2,1)} %copy.88), channel_id=1, replica_groups=mesh['blk'=2,'head'=4,'weight'=4] {'head'}, dimensions={0} | all-to-all | bytes 393216 | tf_op jit(solution)/shard_map/all_to_all | solution.py:130
  145.3 9.5 %all_gather.22 = bf16[256,2,768]{2,1,0:T(2,128)(2,1)} all-gather(bf16[64,2,768]{2,1,0:T(2,128)(2,1)} %reshape.355), channel_id=1, replica_groups=mesh['blk'=2,'head'=4,'weight'=4] {'weight'}, dimensions={0}, use_global_device_ids=true | all-gather | bytes 983040 | tf_op jit(solution)/shard_map/all_gather | solution.py:145
  174.6 26.6 %all-reduce.10.cloned.1.call-done = bf16[256,2,768]{2,1,0:T(2,128)(2,1)} async-done(((bf16[256,2,768]{2,1,0:T(2,128)(2,1)}), bf16[256,2,768]{2,1,0:T(2,128)(2,1)}) %all-reduce.10.cloned.1.call-update) | async-done | bytes 786448
  212.0 9.3 %all_gather.25 = bf16[256,2,768]{2,1,0:T(2,128)(2,1)} all-gather(bf16[64,2,768]{2,1,0:T(2,128)(2,1)} %reshape.360), channel_id=1, replica_groups=mesh['blk'=2,'head'=4,'weight'=4] {'weight'}, dimensions={0}, use_global_device_ids=true | all-gather | bytes 983040 | tf_op jit(solution)/shard_map/all_gather | solution.py:175
  224.3 3.8 fusion.69
  234.2 35.0 %all-reduce.12.cloned.1.call-done = bf16[256,2,768]{2,1,0:T(2,128)(2,1)} async-done(((bf16[256,2,768]{2,1,0:T(2,128)(2,1)}), bf16[256,2,768]{2,1,0:T(2,128)(2,1)}) %all-reduce.12.cloned.1.call-update) | async-done | bytes 786448
  284.3 11.5 %all_to_all.65 = bf16[4,2,12288]{2,1,0:T(2,128)(2,1)} all-to-all(bf16[4,2,12288]{2,1,0:T(2,128)(2,1)} %reshape.380), channel_id=1, replica_groups=mesh['blk'=2,'head'=4,'weight'=4] {'head'}, dimensions={0} | all-to-all | bytes 393216 | tf_op jit(solution)/shard_map/all_to_all | solution.py:212
  305.5 8.9 %all_gather.24 = bf16[2048,2,3]{0,2,1:T(4,128)(2,1)S(1)} all-gather(bf16[256,2,3]{0,2,1:T(4,128)(2,1)S(1)} %bitcast_convert_fusion.6), channel_id=1, replica_groups=mesh['blk'=2,'head'=4,'weight'=4] {'blk','weight'}, dimensions={0}, use_global_device_ids=true | all-gather | bytes 27648 | tf_op jit(solution)/shard_map/all_gather | solution.py:282
  316.2 8.6 %all_gather.27 = bf16[2048,2,3]{0,2,1:T(4,128)(2,1)S(1)} all-gather(bf16[256,2,3]{0,2,1:T(4,128)(2,1)S(1)} %multiply_reduce_fusion.2), channel_id=1, replica_groups=mesh['blk'=2,'head'=4,'weight'=4] {'blk','weight'}, dimensions={0}, use_global_device_ids=true | all-gather | bytes 27648 | tf_op jit(solution)/shard_map/all_gather | solution.py:279
  327.4 38.4 %while.38 = (s32[]{:T(128)}, f32[256,2,3,64]{0,3,2,1:T(8,128)}, f32[256,2,3,64]{0,3,2,1:T(8,128)}, bf16[2048,2,192]{0,2,1:T(8,128)(2,1)}, bf16[2048,2,3,64]{0,3,...) while((s32[]{:T(128)}, f32[256,2,3,64]{0,3,2,1:T(8,128)}, ...), condition=%wide.region_15.16_spmd.clone, body=%wide.region_14.15_spmd.clone.sunk | while | flops 1018921472 | bytes 103770656 | solution.py:53
  329.0 3.7 select_divide_fusion.2
  340.1 3.7 fusion.133
  348.1 3.7 select_divide_fusion.2
  355.5 3.8 fusion.132
  359.3 3.7 fusion.133
  374.6 29.7 %reduce-scatter.2.cloned.1.call-done = bf16[256,2,192]{0,2,1:T(8,128)(2,1)} async-done(((bf16[2048,2,192]{0,2,1:T(8,128)(2,1)}), bf16[256,2,192]{0,2,1:T(8,128)(2,1)}) %reduce-scatter.2.cloned.1.call-update) | async-done | bytes 196624 | tf_op jit(solution)/shard_map/reduce_scatter | solution.py:287
  409.3 4.6 all-to-all-start.3
  416.9 37.5 %all-to-all-done.3 = bf16[256,2,3,192]{3,1,2,0:T(2,128)(2,1)} async-done(((bf16[256,2,3,192]{3,1,2,0:T(2,128)(2,1)}), bf16[256,2,3,192]{3,1,2,0:T(2,128)(2,1)}, u32[]{:S(2)}, u32[]{:S(2)}) %all-to-all-start.3) | async-done | bytes 589856 | tf_op jit(solution)/shard_map/all_to_all | solution.py:293
  460.7 5.2 convolution_bitcast_fusion
  467.6 19.1 %psum.99 = bf16[768]{0:T(1024)(128)(2,1)S(1)} all-reduce(bf16[768]{0:T(1024)(128)(2,1)S(1)} %copy-done.35), channel_id=1, replica_groups=mesh['blk'=2,'head'=4,'weight'=4] {'blk','head'}, use_global_device_ids=true, to_apply=%region_30.31 | all-reduce | flops 768 | bytes 3072 | tf_op jit(solution)/shard_map/psum | solution.py:318
  487.3 45.9 %all-reduce.16.cloned.1.call-done = (bf16[768,768]{1,0:T(8,128)(2,1)}, bf16[768,768]{1,0:T(8,128)(2,1)}) async-done(((bf16[768,768]{1,0:T(8,128)(2,1)}, bf16[768,768]{1,0:T(8,128)(2,1)}), (bf16[768,768]{1,0:T(8,128)(2,1)}, bf16[768,768]{1,0:T(8,128)(2,1)})) %all-reduce.16.cloned.1.call-update) | async-done | bytes 2359312 | tf_op jit(solution)/shard_map/psum | solution.py:317
  546.5 42.4 %all-reduce.2 = (f32[768]{0:T(1024)}, f32[768]{0:T(1024)}, f32[768]{0:T(1024)}, f32[768]{0:T(1024)}, f32[768]{0:T(1024)}, /*index=5*/f32[768]{0:T(1024)}, f32[768]{0:T(1024)}, f32[768]{0:T(1024)}) all-reduce(f32[768]{0:T(1024)} %slice.53, f32[768]{0:T(1024)} %slice.55, ...), channel_id=1, replica_groups=mesh['blk'=2,'head'=4,'weight'=4] {'blk','head','weight'}, use_global_device_ids=true, to_apply=%region_19.20 | all-reduce | flops 6144 | bytes 49152 | tf_op jit(solution)/shard_map/psum | solution.py:301
  588.9 142.2 %all-reduce.14.cloned.1.call-done = (f32[768,2304]{0,1:T(8,128)}, f32[768,768]{1,0:T(8,128)}) async-done(((f32[768,2304]{0,1:T(8,128)}, f32[768,768]{1,0:T(8,128)}), (f32[768,2304]{0,1:T(8,128)}, f32[768,768]{1,0:T(8,128)})) %all-reduce.14.cloned.1.call-update) | async-done | bytes 9437200 | tf_op jit(solution)/shard_map/psum | solution.py:301
  731.1 8.0 %copy.99 = f32[768,2304]{1,0:T(8,128)} copy(f32[768,2304]{0,1:T(8,128)} %get-tuple-element.630) | data formatting | bytes 14155776
  (237 shorter events, 173.7 us)
Async XLA Ops:
  7.2 83.1 %all-gather.4.cloned.1.call-start = ((), (), s32[]{:S(2)}) async-start(), calls=%async_computation.5 | async-start | bytes 4718592 | tf_op jit(solution)/shard_map/all_gather | solution.py:127
  54.4 146.7 %all-reduce.10.cloned.1.call-start = ((), (), s32[]{:S(2)}) async-start(), calls=%async_computation.9 | async-start | bytes 1572864
  136.9 5.9 copy-start.25
  136.9 5.9 copy-start.27
  143.6 14.1 %copy-start.38 = (f32[768]{0:T(1024)S(1)}, f32[768]{0:T(1024)}, u32[]{:S(2)}) copy-start(f32[768]{0:T(1024)} %param.29) | copy-start | bytes 9220
  157.7 4.5 copy-start.36
  163.9 4.9 copy-start.26
  166.8 102.4 %all-reduce.12.cloned.1.call-start = ((), (), s32[]{:S(2)}) async-start(), calls=%async_computation.10 | async-start | bytes 1572864
  224.3 4.7 copy-start.37
  233.6 91.8 %all-gather.6.cloned.1.call-start = ((), (), s32[]{:S(2)}) async-start(), calls=%async_computation.6 | async-start | bytes 1769472 | tf_op jit(solution)/shard_map/all_gather | solution.py:277
  234.1 92.0 %all-gather.8.cloned.1.call-start = ((), (), s32[]{:S(2)}) async-start(), calls=%async_computation.7 | async-start | bytes 1769472 | tf_op jit(solution)/shard_map/all_gather | solution.py:278
  273.0 4.4 copy-start.18
  301.9 102.4 %reduce-scatter.2.cloned.1.call-start = ((), (), s32[]{:S(2)}) async-start(), calls=%async_computation.8 | async-start | bytes 1769472 | tf_op jit(solution)/shard_map/reduce_scatter | solution.py:287
  328.9 3.8 copy-start.3
  328.9 3.8 copy-start.12
  336.3 3.7 copy-start.4
  336.4 3.7 copy-start.5
  340.1 3.8 copy-start.1
  340.1 3.8 copy-start.10
  348.1 3.8 copy-start.3
  348.1 3.8 copy-start.12
  351.9 3.7 copy-start.2
  355.5 3.8 copy-start.4
  355.5 3.8 copy-start.5
  359.3 3.8 copy-start.1
  359.3 3.8 copy-start.10
  365.9 167.4 %all-reduce.16.cloned.1.call-start = ((), (), s32[]{:S(2)}) async-start(), calls=%async_computation.12 | async-start | bytes 4718592 | tf_op jit(solution)/shard_map/psum | solution.py:317
  409.3 45.2 %all-to-all-start.3 = ((bf16[256,2,3,192]{3,1,2,0:T(2,128)(2,1)}), bf16[256,2,3,192]{3,1,2,0:T(2,128)(2,1)}, u32[]{:S(2)}, u32[]{:S(2)}) async-start(bf16[256,2,3,192]{3,1,2,0:T(2,128)(2,1)} %copy.96), calls=%async_computation.4 | async-start | bytes 1572864 | tf_op jit(solution)/shard_map/all_to_all | solution.py:293
  413.9 317.2 %all-reduce.14.cloned.1.call-start = ((), (), s32[]{:S(2)}) async-start(), calls=%async_computation.11 | async-start | bytes 18874368 | tf_op jit(solution)/shard_map/psum | solution.py:301
  539.8 6.6 copy-start.28
  539.8 6.6 copy-start.29
  539.8 6.6 copy-start.30
  (31 other events, 57.6 us)
Sparse Core Ops, SparseCore 0:
  54.6 35.6 all-gather.3
  166.9 34.1 all-reduce.9
  233.7 35.4 all-reduce.11
  270.9 25.7 all-gather.5
  302.0 24.0 all-gather.7
  366.0 38.2 reduce-scatter.1
  408.4 124.7 all-reduce.15
  539.8 191.2 all-reduce.13
where the time goes:
time: 752 us; the launch traced here: 749 us
  waiting for transfers between devices  350 us (47%)
  blocking collectives  146 us (19%)
  local copies, waits for them, and re-layouts  118 us (16%)
  matrix products  79.5 us (11%)
  other arithmetic  35 us (5%)
  between operations  15.1 us (2%)
    psum x1, waiting for transfers between devices, per_device(): lax.psum((grad_qkv_weight, column_sums[:width], column_sums[2 * width:],...  142 us
    unnamed x10, waiting for transfers between devices  62.2 us
    psum x1, waiting for transfers between devices, per_device(): lax.psum(grad_up_weight.astype(jnp.bfloat16), ('blk', 'head'))  45.9 us
    psum x1, blocking collectives, per_device(): lax.psum((grad_qkv_weight, column_sums[:width], column_sums[2 * width:],...  42.4 us
    all_to_all x1, waiting for transfers between devices, per_device(): lax.all_to_all(stacked, 'head', split_axis=0, concat_axis=3, tiled=True)  37.5 us
    unnamed x68, local copies, waits for them, and re-layouts  34.1 us
    all_gather x1, waiting for transfers between devices, per_device(): lax.all_gather(keyval, ('blk', 'weight'), axis=0, tiled=True)  32 us
    reduce_scatter x1, waiting for transfers between devices, per_device(): lax.psum_scatter(query_sums.astype(jnp.bfloat16), ('blk', 'weight'), scat...  29.7 us
  transfers between devices with their start and end apart: 9, of which 8 were waited for; matrix products, arithmetic and copies ran while one was open for 11% of the time, Pallas kernels for 0%

commit v1 on v0

--- a/solution.py
+++ b/solution.py
@@ -314,7 +314,7 @@
         ("blk", "head", "weight"),
     )
     hidden_sums = (
-        lax.psum(grad_up_weight.astype(jnp.bfloat16), ("blk", "head")).astype(jnp.float32),
+        lax.psum(lax.psum(grad_up_weight.astype(jnp.bfloat16), "blk"), "head").astype(jnp.float32),
         lax.psum(grad_up_bias.astype(jnp.bfloat16), ("blk", "head")).astype(jnp.float32),
         lax.psum(grad_down_weight.astype(jnp.bfloat16), ("blk", "head")).astype(jnp.float32),
     )

time: 752 us -> 809 us (1.076)
  waiting for transfers between devices: 350 us -> 405 us
    psum x1 -> x3, waiting for transfers between devices: 45.9 us -> 137 us  [the longest x1 54.7 us: per_device(): lax.psum(lax.psum(grad_up_weight.astype(jnp.bfloat16), 'blk'), 'head')]
    all_to_all x1, waiting for transfers between devices: 37.5 us -> 0.01 us  [per_device(): lax.all_to_all(stacked, 'head', split_axis=0, concat_axis=3, tiled=True)]
    unnamed x68 -> x60, local copies, waits for them, and re-layouts: 34.1 us -> 34.7 us
    unnamed x10 -> x12, waiting for transfers between devices: 62.2 us -> 62.3 us
  transfers between devices with their start and end apart: 9 -> 11, of which waited for: 8 -> 9; matrix products, arithmetic and copies ran while one was open for 11% -> 10% of each run, Pallas kernels for 0% -> 0%
where the time goes in v1:
time: 809 us; the launch traced here: 806 us
  waiting for transfers between devices  405 us (50%)
  blocking collectives  148 us (18%)
  local copies, waits for them, and re-layouts  118 us (15%)
  matrix products  79.5 us (10%)
  other arithmetic  35.2 us (4%)
  between operations  15.1 us (2%)
    psum x1, waiting for transfers between devices, per_device(): lax.psum((grad_qkv_weight, column_sums[:width], column_sums[2 * width:],...  145 us
    unnamed x12, waiting for transfers between devices  62.3 us
    psum x1, waiting for transfers between devices, per_device(): lax.psum(lax.psum(grad_up_weight.astype(jnp.bfloat16), 'blk'), 'head')  54.7 us
    psum x1, waiting for transfers between devices, per_device(): lax.psum(grad_down_weight.astype(jnp.bfloat16), ('blk', 'head'))  45.6 us
    psum x1, blocking collectives, per_device(): lax.psum((grad_qkv_weight, column_sums[:width], column_sums[2 * width:],...  43.3 us
    psum x1, waiting for transfers between devices, per_device(): lax.psum(grad_up_weight.astype(jnp.bfloat16), 'blk')  36.3 us
    unnamed x60, local copies, waits for them, and re-layouts  34.7 us
    all_gather x1, waiting for transfers between devices, per_device(): lax.all_gather(keyval, ('blk', 'weight'), axis=0, tiled=True)  32 us
  transfers between devices with their start and end apart: 11, of which 9 were waited for; matrix products, arithmetic and copies ran while one was open for 10% of the time, Pallas kernels for 0%

profile of v1, /device:TPU:0, one launch (start us, length us, event | category | flops | bytes accessed | tf_op | source)
XLA Modules:
  0.0 806.2 jit_solution(9666604094240128776)
XLA Ops:
  14.1 4.8 copy.83
  21.6 22.3 %all_to_all.63 = bf16[4,2,36864]{2,1,0:T(2,128)(2,1)} all-to-all(bf16[4,2,36864]{2,1,0:T(2,128)(2,1)} %reshape.378), channel_id=1, replica_groups=mesh['blk'=2,'head'=4,'weight'=4] {'head'}, dimensions={0} | all-to-all | bytes 1179648 | tf_op jit(solution)/shard_map/all_to_all | solution.py:87
  46.6 4.8 copy.101
  58.3 32.0 %all-gather.4.cloned.1.call-done = bf16[2048,2,2,192]{3,0,2,1:T(8,128)(2,1)} async-done(((bf16[256,2,2,192]{3,0,2,1:T(8,128)(2,1)}), bf16[2048,2,2,192]{3,0,2,1:T(8,128)(2,1)}) %all-gather.4.cloned.1.call-update) | async-done | bytes 3145744 | tf_op jit(solution)/shard_map/all_gather | solution.py:127
  90.3 6.1 copy.87
  96.4 23.1 %while.37 = (s32[]{:T(128)}, f32[256,2,3,64]{0,3,2,1:T(8,128)}, f32[2,3,256]{2,1,0:T(4,128)S(1)}, bf16[2048,2,2,192]{0,3,1,2:T(8,128)(2,1)}, s32[2]{0:T(128)}, /...) while((s32[]{:T(128)}, f32[256,2,3,64]{0,3,2,1:T(8,128)}, ...), condition=%wide.region_2.3_spmd.clone, body=%wide.region_0.2_spmd.clone.sunk | while | flops 412356096 | bytes 19118332 | solution.py:53
  103.0 4.8 fusion.121
  114.6 4.9 fusion.121
  123.0 13.9 %all_to_all.64 = bf16[256,2,192]{2,1,0:T(2,128)(2,1)S(1)} all-to-all(bf16[256,2,192]{2,1,0:T(2,128)(2,1)} %copy.88), channel_id=1, replica_groups=mesh['blk'=2,'head'=4,'weight'=4] {'head'}, dimensions={0} | all-to-all | bytes 393216 | tf_op jit(solution)/shard_map/all_to_all | solution.py:130
  145.3 9.5 %all_gather.22 = bf16[256,2,768]{2,1,0:T(2,128)(2,1)} all-gather(bf16[64,2,768]{2,1,0:T(2,128)(2,1)} %reshape.355), channel_id=1, replica_groups=mesh['blk'=2,'head'=4,'weight'=4] {'weight'}, dimensions={0}, use_global_device_ids=true | all-gather | bytes 983040 | tf_op jit(solution)/shard_map/all_gather | solution.py:145
  174.5 26.6 %all-reduce.17.cloned.1.call-done = bf16[256,2,768]{2,1,0:T(2,128)(2,1)} async-done(((bf16[256,2,768]{2,1,0:T(2,128)(2,1)}), bf16[256,2,768]{2,1,0:T(2,128)(2,1)}) %all-reduce.17.cloned.1.call-update) | async-done | bytes 786448
  212.0 9.3 %all_gather.25 = bf16[256,2,768]{2,1,0:T(2,128)(2,1)} all-gather(bf16[64,2,768]{2,1,0:T(2,128)(2,1)} %reshape.360), channel_id=1, replica_groups=mesh['blk'=2,'head'=4,'weight'=4] {'weight'}, dimensions={0}, use_global_device_ids=true | all-gather | bytes 983040 | tf_op jit(solution)/shard_map/all_gather | solution.py:175
  224.2 3.8 fusion.69
  234.2 35.0 %all-reduce.19.cloned.1.call-done = bf16[256,2,768]{2,1,0:T(2,128)(2,1)} async-done(((bf16[256,2,768]{2,1,0:T(2,128)(2,1)}), bf16[256,2,768]{2,1,0:T(2,128)(2,1)}) %all-reduce.19.cloned.1.call-update) | async-done | bytes 786448
  284.3 11.5 %all_to_all.65 = bf16[4,2,12288]{2,1,0:T(2,128)(2,1)} all-to-all(bf16[4,2,12288]{2,1,0:T(2,128)(2,1)} %reshape.380), channel_id=1, replica_groups=mesh['blk'=2,'head'=4,'weight'=4] {'head'}, dimensions={0} | all-to-all | bytes 393216 | tf_op jit(solution)/shard_map/all_to_all | solution.py:212
  305.5 8.9 %all_gather.24 = bf16[2048,2,3]{0,2,1:T(4,128)(2,1)S(1)} all-gather(bf16[256,2,3]{0,2,1:T(4,128)(2,1)S(1)} %bitcast_convert_fusion.6), channel_id=1, replica_groups=mesh['blk'=2,'head'=4,'weight'=4] {'blk','weight'}, dimensions={0}, use_global_device_ids=true | all-gather | bytes 27648 | tf_op jit(solution)/shard_map/all_gather | solution.py:282
  316.2 8.6 %all_gather.27 = bf16[2048,2,3]{0,2,1:T(4,128)(2,1)S(1)} all-gather(bf16[256,2,3]{0,2,1:T(4,128)(2,1)S(1)} %multiply_reduce_fusion.2), channel_id=1, replica_groups=mesh['blk'=2,'head'=4,'weight'=4] {'blk','weight'}, dimensions={0}, use_global_device_ids=true | all-gather | bytes 27648 | tf_op jit(solution)/shard_map/all_gather | solution.py:279
  327.4 37.1 %while.38 = (s32[]{:T(128)}, f32[256,2,3,64]{0,3,2,1:T(8,128)}, f32[256,2,3,64]{0,3,2,1:T(8,128)}, bf16[2048,2,192]{0,2,1:T(8,128)(2,1)}, bf16[2048,2,3,64]{0,3,...) while((s32[]{:T(128)}, f32[256,2,3,64]{0,3,2,1:T(8,128)}, ...), condition=%wide.region_15.16_spmd.clone, body=%wide.region_14.15_spmd.clone.sunk | while | flops 1018921472 | bytes 88041880 | solution.py:53
  329.0 3.7 select_divide_fusion.2
  341.7 4.3 fusion.133
  347.5 3.7 select_divide_fusion.2
  360.3 4.3 fusion.133
  374.6 28.4 %reduce-scatter.2.cloned.1.call-done = bf16[256,2,192]{0,2,1:T(8,128)(2,1)} async-done(((bf16[2048,2,192]{0,2,1:T(8,128)(2,1)}), bf16[256,2,192]{0,2,1:T(8,128)(2,1)}) %reduce-scatter.2.cloned.1.call-update) | async-done | bytes 196624 | tf_op jit(solution)/shard_map/reduce_scatter | solution.py:287
  408.0 4.6 all-to-all-start.3
  412.6 36.3 %all-reduce.11.cloned.1.call-done = bf16[768,768]{1,0:T(8,128)(2,1)} async-done(((bf16[768,768]{1,0:T(8,128)(2,1)}), bf16[768,768]{1,0:T(8,128)(2,1)}) %all-reduce.11.cloned.1.call-update) | async-done | bytes 1179664 | tf_op jit(solution)/shard_map/psum | solution.py:317
  458.2 5.2 convolution_bitcast_fusion
  464.1 20.8 %psum.107 = bf16[768]{0:T(1024)(128)(2,1)S(1)} all-reduce(bf16[768]{0:T(1024)(128)(2,1)S(1)} %copy-done.28), channel_id=1, replica_groups=mesh['blk'=2,'head'=4,'weight'=4] {'blk','head'}, use_global_device_ids=true, to_apply=%region_31.32 | all-reduce | flops 768 | bytes 3072 | tf_op jit(solution)/shard_map/psum | solution.py:318
  487.1 45.6 %all-reduce.15.cloned.1.call-done = bf16[768,768]{1,0:T(8,128)(2,1)} async-done(((bf16[768,768]{1,0:T(8,128)(2,1)}), bf16[768,768]{1,0:T(8,128)(2,1)}) %all-reduce.15.cloned.1.call-update) | async-done | bytes 1179664 | tf_op jit(solution)/shard_map/psum | solution.py:319
  535.6 54.7 %all-reduce.13.cloned.1.call-done = bf16[768,768]{1,0:T(8,128)(2,1)} async-done(((bf16[768,768]{1,0:T(8,128)(2,1)}), bf16[768,768]{1,0:T(8,128)(2,1)}) %all-reduce.13.cloned.1.call-update) | async-done | bytes 1179664 | tf_op jit(solution)/shard_map/psum | solution.py:317
  599.9 43.3 %all-reduce.2 = (f32[768]{0:T(1024)}, f32[768]{0:T(1024)}, f32[768]{0:T(1024)}, f32[768]{0:T(1024)}, f32[768]{0:T(1024)}, /*index=5*/f32[768]{0:T(1024)}, f32[768]{0:T(1024)}, f32[768]{0:T(1024)}) all-reduce(f32[768]{0:T(1024)} %slice.53, f32[768]{0:T(1024)} %slice.55, ...), channel_id=1, replica_groups=mesh['blk'=2,'head'=4,'weight'=4] {'blk','head','weight'}, use_global_device_ids=true, to_apply=%region_19.20 | all-reduce | flops 6144 | bytes 49152 | tf_op jit(solution)/shard_map/psum | solution.py:301
  643.2 145.0 %all-reduce.21.cloned.1.call-done = (f32[768,2304]{0,1:T(8,128)}, f32[768,768]{1,0:T(8,128)}) async-done(((f32[768,2304]{0,1:T(8,128)}, f32[768,768]{1,0:T(8,128)}), (f32[768,2304]{0,1:T(8,128)}, f32[768,768]{1,0:T(8,128)})) %all-reduce.21.cloned.1.call-update) | async-done | bytes 9437200 | tf_op jit(solution)/shard_map/psum | solution.py:301
  788.2 8.0 copy.99
  (219 shorter events, 176.3 us)
Async XLA Ops:
  7.2 83.1 %all-gather.4.cloned.1.call-start = ((), (), s32[]{:S(2)}) async-start(), calls=%async_computation.5 | async-start | bytes 4718592 | tf_op jit(solution)/shard_map/all_gather | solution.py:127
  54.4 146.7 %all-reduce.17.cloned.1.call-start = ((), (), s32[]{:S(2)}) async-start(), calls=%async_computation.12 | async-start | bytes 1572864
  96.4 3.2 copy-start.16
  99.5 3.5 copy-start.17
  107.9 3.2 copy-start.16
  111.1 3.5 copy-start.17
  136.9 5.9 copy-start.18
  136.9 5.8 copy-start.20
  143.6 14.1 %copy-start.31 = (f32[768]{0:T(1024)S(1)}, f32[768]{0:T(1024)}, u32[]{:S(2)}) copy-start(f32[768]{0:T(1024)} %param.29) | copy-start | bytes 9220
  157.7 4.5 copy-start.29
  163.8 4.9 copy-start.19
  166.7 102.5 %all-reduce.19.cloned.1.call-start = ((), (), s32[]{:S(2)}) async-start(), calls=%async_computation.13 | async-start | bytes 1572864
  224.2 4.7 copy-start.30
  233.5 91.9 %all-gather.6.cloned.1.call-start = ((), (), s32[]{:S(2)}) async-start(), calls=%async_computation.6 | async-start | bytes 1769472 | tf_op jit(solution)/shard_map/all_gather | solution.py:277
  234.1 92.0 %all-gather.8.cloned.1.call-start = ((), (), s32[]{:S(2)}) async-start(), calls=%async_computation.7 | async-start | bytes 1769472 | tf_op jit(solution)/shard_map/all_gather | solution.py:278
  273.0 4.4 copy-start.13
  301.9 101.1 %reduce-scatter.2.cloned.1.call-start = ((), (), s32[]{:S(2)}) async-start(), calls=%async_computation.8 | async-start | bytes 1769472 | tf_op jit(solution)/shard_map/reduce_scatter | solution.py:287
  329.0 3.8 copy-start.3
  329.0 3.8 copy-start.10
  338.0 3.7 copy-start.4
  347.5 3.8 copy-start.3
  347.5 3.8 copy-start.10
  356.5 3.7 copy-start.4
  364.6 84.3 %all-reduce.11.cloned.1.call-start = ((), (), s32[]{:S(2)}) async-start(), calls=%async_computation.9 | async-start | bytes 2359296 | tf_op jit(solution)/shard_map/psum | solution.py:317
  367.9 164.9 %all-reduce.15.cloned.1.call-start = ((), (), s32[]{:S(2)}) async-start(), calls=%async_computation.11 | async-start | bytes 2359296 | tf_op jit(solution)/shard_map/psum | solution.py:319
  408.0 44.0 %all-to-all-start.3 = ((bf16[256,2,3,192]{3,1,2,0:T(2,128)(2,1)}), bf16[256,2,3,192]{3,1,2,0:T(2,128)(2,1)}, u32[]{:S(2)}, u32[]{:S(2)}) async-start(bf16[256,2,3,192]{3,1,2,0:T(2,128)(2,1)} %copy.96), calls=%async_computation.4 | async-start | bytes 1572864 | tf_op jit(solution)/shard_map/all_to_all | solution.py:293
  412.6 177.7 %all-reduce.13.cloned.1.call-start = ((), (), s32[]{:S(2)}) async-start(), calls=%async_computation.10 | async-start | bytes 2359296 | tf_op jit(solution)/shard_map/psum | solution.py:317
  448.9 339.3 %all-reduce.21.cloned.1.call-start = ((), (), s32[]{:S(2)}) async-start(), calls=%async_computation.14 | async-start | bytes 18874368 | tf_op jit(solution)/shard_map/psum | solution.py:301
  590.3 2.9 copy-start.9
  594.7 5.2 copy-start.21
  594.7 5.2 copy-start.22
  594.7 5.2 copy-start.23
  (21 other events, 33.3 us)
Sparse Core Ops, SparseCore 0:
  54.6 35.6 all-gather.3
  166.8 34.2 all-reduce.16
  233.7 35.4 all-reduce.18
  270.9 25.7 all-gather.5
  302.0 24.0 all-gather.7
  364.7 38.2 reduce-scatter.1
  405.9 42.9 all-reduce.10
  452.3 80.3 all-reduce.14
  535.1 55.1 all-reduce.12
  596.7 191.4 all-reduce.20
